TPU v7x, 32 devices: a whole 2x2x4 slice. The times are simulated.
32 devices in a mesh: stn: 4 (over z), chan: 8 (over y, x, core).
Axes of the slice: x: 2, y: 2, z: 4, core: 2. Of those that a mesh axis runs over, the one named last changes fastest.
Arguments:
- voltages: bfloat16 [1024, 8, 8, 1024], P('stn', 'chan'), may hold values from -6 to 6
- fir_taps: float32 [8, 8, 1024], replicated, may hold values from -2.5 to 2.5
Outputs:
- visibilities: float32 [4, 64, 2, 1024, 1024], P(None, 'chan', None, 'stn')
All inputs are finite; a program needn't handle non-finite values.
Results may differ from a plain program's by a relative error of at most 0.0044.
Values may be sent and summed in bfloat16 or wider, within the bound.
No kernel may reach another device: no remote copies, remote signals or barrier semaphores. Data moves between devices by JAX's collectives and lax.ppermute only.
A program may use at most 192 MiB of HBM per device.

v0:
```python
import math
import jax
import jax.numpy as jnp
from jax import lax
from jax.sharding import PartitionSpec as P

AVG = 16


def shifted(block, axis, distance):
    devices = range(lax.axis_size(axis))
    route = [(i - distance, i) for i in devices if i - distance in devices]
    return lax.ppermute(block, axis, route)


def rotation(numbers, modulus):
    angles = (numbers % modulus).astype(jnp.float32) * jnp.float32(-2.0 * math.pi / modulus)
    return (jnp.cos(angles), jnp.sin(angles))


def split_pair(table):
    upper = table.astype(jnp.bfloat16)
    lower = (table - upper.astype(jnp.float32)).astype(jnp.bfloat16)
    return (upper, lower)


def complex_table(real_part, imag_part, axis_at):
    first = jnp.stack([real_part, imag_part], axis=-1)
    second = jnp.stack([-imag_part, real_part], axis=-1)
    return jnp.stack([first, second], axis=axis_at)


def per_device(voltages, fir_taps):
    inputs_dev, _, frames_dev, slot_count = voltages.shape
    phases = fir_taps.shape[0]
    tap_count = fir_taps.shape[1]
    lane_count = lax.axis_size("chan")
    groups = lane_count // phases
    position = lax.axis_index("chan")
    my_phase = position % phases
    my_group = position // phases
    recent = voltages[:, 0]
    if groups > 1:
        earlier = shifted(voltages[:, 0, frames_dev - (tap_count - 1) :, :], "chan", phases)
    else:
        earlier = jnp.zeros((inputs_dev, tap_count - 1, slot_count), voltages.dtype)
    series = jnp.concatenate([earlier, recent], axis=1)
    coeffs = lax.dynamic_index_in_dim(fir_taps, my_phase, 0, keepdims=False)
    frame_ids = my_group * frames_dev + jnp.arange(frames_dev, dtype=jnp.int32)
    keep_mask = (frame_ids >= tap_count - 1).astype(jnp.float32)
    filtered = sum(
        (
            coeffs[tap_index]
            * series[:, tap_count - 1 - tap_index : tap_count - 1 - tap_index + frames_dev].astype(
                jnp.float32
            )
            for tap_index in range(tap_count)
        )
    )
    filtered = filtered * keep_mask[None, :, None]
    better = lax.Precision.HIGH
    split_len = slot_count // phases
    folded = filtered.reshape(inputs_dev, frames_dev, split_len, phases)
    slot_ids = jnp.arange(split_len, dtype=jnp.int32)
    short_re, short_im = rotation(slot_ids[:, None] * slot_ids[None, :], split_len)
    short_table = jnp.stack([short_re, short_im], axis=-1)
    inner = jnp.einsum(
        "ifqr,qvc->rvcfi", folded, short_table, precision=better, preferred_element_type=jnp.float32
    )
    rest_ids = jnp.arange(phases, dtype=jnp.int32)
    freq_ids = jnp.arange(slot_count, dtype=jnp.int32).reshape(phases, split_len)
    twist_re, twist_im = rotation(
        (my_phase + phases * rest_ids)[:, None, None] * freq_ids[None], phases * slot_count
    )
    twist_table = complex_table(twist_re, twist_im, 3)
    branch = jnp.einsum(
        "rvcfi,ruvcd->uvfdi",
        inner,
        twist_table,
        precision=better,
        preferred_element_type=jnp.float32,
    )
    branch = branch.reshape(slot_count, 1, frames_dev, 2, inputs_dev).astype(jnp.bfloat16)
    band_count = phases // 2
    band_re, band_im = rotation(
        rest_ids[:, None] * jnp.arange(band_count, dtype=jnp.int32)[None, :], phases
    )
    band_table = complex_table(band_re, band_im, 1)
    band_upper, band_lower = split_pair(band_table)
    turned = lax.all_to_all(branch, "chan", split_axis=0, concat_axis=1, tiled=True)
    span_len = turned.shape[0]
    sources = turned.shape[1]
    item_count = turned.shape[2]
    grouped = turned.reshape(span_len, sources // phases, phases, item_count, 2, inputs_dev)
    phase_form = "wgpfci,pcbd->bwgfdi"
    total = jnp.einsum(
        phase_form, grouped, band_upper, preferred_element_type=jnp.float32
    ) + jnp.einsum(phase_form, grouped, band_lower, preferred_element_type=jnp.float32)
    spectra = total.astype(jnp.bfloat16)
    span_dev = spectra.shape[1]
    subs_dev = span_dev // AVG
    stacked = spectra.reshape(band_count, subs_dev, AVG * groups * frames_dev, 2, inputs_dev)
    columns = stacked.reshape(band_count, subs_dev, -1, inputs_dev)
    swapped = jnp.stack([stacked[:, :, :, 1], -stacked[:, :, :, 0]], axis=3).reshape(
        band_count, subs_dev, -1, inputs_dev
    )
    left_side = jnp.stack([columns, swapped], axis=2)
    spectra_count = groups * frames_dev - (tap_count - 1)
    scaling = 1.0 / (phases * slot_count * AVG * spectra_count)
    vis_form = "bsokn,bskw->bsonw"
    return (
        jnp.einsum(
            vis_form,
            left_side,
            lax.all_gather(columns, "stn", axis=3, tiled=True),
            preferred_element_type=jnp.float32,
        )
        * scaling
    )


def solution(mesh):
    return jax.shard_map(
        per_device,
        mesh=mesh,
        in_specs=(P("stn", "chan", None, None), P()),
        out_specs=P(None, "chan", None, "stn", None),
        check_vma=False,
    )
```

profile of v0, /device:TPU:0, one launch (start us, length us, event | category | flops | bytes accessed | tf_op | source)
XLA Modules:
  0.0 559.5 jit_solution(15071491346341078132)
XLA Ops:
  6.5 0.3 fusion.36
  6.9 0.2 fusion.38
  7.1 0.5 copy.40
  7.6 0.5 copy.41
  8.1 6.9 %copy.42 = bf16[256,1,8,1024]{0,3,2,1:T(8,128)(2,1)} copy(bf16[256,1,8,1024]{3,2,1,0:T(8,128)(2,1)} %param.2) | data formatting | bytes 8388608 | tf_op args[0]
  15.0 1.1 constant_dynamic-slice_fusion.6
  16.1 12.6 %multiply_bitcast_fusion = f32[256,8,128,8]{0,3,2,1:T(8,128)} fusion(bf16[256,8,1024]{0,2,1:T(8,128)(2,1)} %bitcast.96, f32[8]{0:T(128)S(1)} %compare_convert_fusion, f32[1024]{0:T(1024)S(1)} %bitcast.107, f32[1024]{0:T(1024)S(1)} %bitcast.101, f32[1024]{0:T(1024)S(1)} %bitcast.102, f32[1024]{0:T(1024)S(1)} %bitcast.103, f32[1024]{0:T(1024)S(1)} %bitcast.104, ...), kind=kLoop, calls=%fused_computation.24 | loop fusion | flops 50331648 | bytes 12615712 | tf_op jit(solution)/shard_map/reshape | solution.py:63
  28.7 9.1 %copy.44 = f32[256,8,128,8]{2,0,3,1:T(8,128)} copy(f32[256,8,128,8]{0,3,2,1:T(8,128)} %multiply_bitcast_fusion) | data formatting | bytes 16777216 | tf_op jit(solution)/shard_map/reshape | solution.py:63
  37.8 14.2 %fusion.18 = f32[8,128,2,8,256,1]{4,1,0,3,2,5:T(8,128)} fusion(f32[256,8,128,8]{2,0,3,1:T(8,128)} %copy.44, f32[128,128,1]{1,0,2:T(8,128)S(1)} %get-tuple-element.24, f32[128,128,1]{1,0,2:T(8,128)S(1)} %get-tuple-element.25), kind=kOutput, calls=%fused_computation.27 | convolution fusion | flops 3221258240 | bytes 25296896 | tf_op jit(solution)/shard_map/ifqr,qvc->rvcfi/dot_general | solution.py:67
  52.0 25.0 %fusion.3 = bf16[8,128,8,2,256]{4,0,2,3,1:T(8,128)(2,1)} fusion(f32[8,128,2,8,256,1]{4,1,0,3,2,5:T(8,128)} %fusion.18, f32[8,8,128,1,2]{0,1,3,4,2:T(8,128)S(1)} %bitcast.99, f32[8,8,128,1,2]{0,1,3,4,2:T(8,128)S(1)} %bitcast.98), kind=kOutput, calls=%fused_computation.12 | convolution fusion | flops 406880256 | bytes 25296896 | tf_op jit(solution)/shard_map/rvcfi,ruvcd->uvfdi/dot_general | solution.py:76
  77.0 8.5 %copy.46 = bf16[8,128,8,2,256]{4,2,3,1,0:T(8,128)(2,1)} copy(bf16[8,128,8,2,256]{4,0,2,3,1:T(8,128)(2,1)} %fusion.3) | data formatting | bytes 16777216 | tf_op jit(solution)/shard_map/convert_element_type | solution.py:83
  85.5 16.0 %all-to-all-start = ((bf16[1024,1,8,2,256]{4,2,3,1,0:T(8,128)(2,1)}), bf16[1024,1,8,2,256]{4,2,3,1,0:T(8,128)(2,1)}, u32[]{:S(2)}, u32[]{:S(2)}) async-start(bf16[1024,1,8,2,256]{4,2,3,1,0:T(8,128)(2,1)} %bitcast.95), calls=%async_computation | async-start | bytes 16777216 | tf_op jit(solution)/shard_map/all_to_all | solution.py:90
  101.5 0.0 all-gather.2.cloned.1.call-start
  101.6 0.1 fusion.52
  101.6 0.1 fusion.50
  101.7 94.6 %all-to-all-done = bf16[1024,1,8,2,256]{4,2,3,1,0:T(8,128)(2,1)} async-done(((bf16[1024,1,8,2,256]{4,2,3,1,0:T(8,128)(2,1)}), bf16[1024,1,8,2,256]{4,2,3,1,0:T(8,128)(2,1)}, u32[]{:S(2)}, u32[]{:S(2)}) %all-to-all-start) | async-done | bytes 8388640 | tf_op jit(solution)/shard_map/all_to_all | solution.py:90
  196.3 12.6 %fusion.8 = f32[4,2,128,8,256,1]{4,0,5,3,2,1:T(4,128)} fusion(bf16[8,128,1,8,2,256]{5,3,4,2,1,0:T(8,128)(2,1)} %bitcast.28, f32[8,1,4,2]{0,2,1,3:T(4,128)S(1)} %get-tuple-element.21, f32[8,1,4,2]{0,2,1,3:T(4,128)S(1)} %get-tuple-element.20), kind=kOutput, calls=%fused_computation.18 | convolution fusion | flops 67109504 | bytes 16777728 | tf_op jit(solution)/shard_map/wgpfci,pcbd->bwgfdi/dot_general | solution.py:98
  208.9 16.7 %fusion.7 = bf16[4,2,128,8,256]{4,0,3,2,1:T(4,128)(2,1)} fusion(f32[4,2,128,8,256,1]{4,0,5,3,2,1:T(4,128)} %fusion.8, bf16[8,128,1,8,2,256]{5,3,4,2,1,0:T(8,128)(2,1)} %bitcast.28, f32[8,1,4,2]{0,2,1,3:T(4,128)S(1)} %get-tuple-element.21, f32[8,1,4,2]{0,2,1,3:T(4,128)S(1)} %get-tuple-element.20), kind=kOutput, calls=%fused_computation.17 | convolution fusion | flops 71303680 | bytes 20972032 | tf_op jit(solution)/shard_map/wgpfci,pcbd->bwgfdi/dot_general | solution.py:96
  225.6 4.3 copy.48
  229.9 0.0 copy-start
  229.9 1.9 copy-done
  231.8 2.8 copy.54
  234.6 0.0 all-gather.2.cloned.1.call-update
  234.6 7.5 %copy.51 = bf16[4,8,1,256,256]{3,4,2,1,0:T(8,128)(2,1)} copy(bf16[4,8,1,256,256]{4,0,3,1,2:T(4,128)(2,1)} %bitcast.94) | data formatting | bytes 8388608 | tf_op jit(solution)/shard_map/stack;reshape;reshape | solution.py:107
  242.1 3.8 fusion.58
  245.9 1.2 copy.68
  247.1 2.4 copy_negate_fusion
  249.5 2.3 pad_maximum_fusion
  251.8 7.6 %copy.52 = bf16[4,8,1,256,256]{3,4,2,1,0:T(8,128)(2,1)} copy(bf16[4,8,1,256,256]{4,1,3,0,2:T(8,128)(2,1)} %bitcast.97) | data formatting | bytes 8388608 | tf_op jit(solution)/shard_map/stack;reshape | solution.py:107
  259.4 261.7 %all-gather.2.cloned.1.call-done = bf16[4,8,256,1024]{3,2,1,0:T(8,128)(2,1)} async-done(((bf16[4,8,256,256]{3,2,1,0:T(8,128)(2,1)}), bf16[4,8,256,1024]{3,2,1,0:T(8,128)(2,1)}) %all-gather.2.cloned.1.call-update) | async-done | bytes 16777232 | tf_op jit(solution)/shard_map/all_gather | solution.py:115
  521.2 31.3 %convolution_multiply_fusion = f32[4,8,2,256,1024]{4,3,2,1,0:T(8,128)} fusion(bf16[4,8,256,1024]{3,2,1,0:T(8,128)(2,1)} %all-gather.2.cloned.1.call-done, bf16[4,8,1,256,256]{3,4,2,1,0:T(8,128)(2,1)} %copy.52, bf16[4,8,1,256,256]{3,4,2,1,0:T(8,128)(2,1)} %copy.51), kind=kOutput, calls=%fused_computation | convolution fusion | flops 8610906112 | bytes 92274688 | tf_op jit(solution)/shard_map/bsokn,bskw->bsonw/dot_general | solution.py:112
  (5 shorter events, 0.0 us)
Async XLA Ops:
  85.5 110.8 %all-to-all-start = ((bf16[1024,1,8,2,256]{4,2,3,1,0:T(8,128)(2,1)}), bf16[1024,1,8,2,256]{4,2,3,1,0:T(8,128)(2,1)}, u32[]{:S(2)}, u32[]{:S(2)}) async-start(bf16[1024,1,8,2,256]{4,2,3,1,0:T(8,128)(2,1)} %bitcast.95), calls=%async_computation | async-start | bytes 16777216 | tf_op jit(solution)/shard_map/all_to_all | solution.py:90
  101.5 419.6 %all-gather.2.cloned.1.call-start = ((), (), s32[]{:S(2)}) async-start(), calls=%async_computation.1 | async-start | bytes 20971520 | tf_op jit(solution)/shard_map/all_gather | solution.py:115
  229.9 2.0 copy-start
Sparse Core Ops, SparseCore 0:
  234.8 286.3 all-gather.1
where the time goes:
time: 566 us; the launch traced here: 560 us
  waiting for transfers between devices  356 us (63%)
  matrix products  99.8 us (18%)
  local copies, waits for them, and re-layouts  55.6 us (10%)
  other arithmetic  18 us (3%)
  starting transfers between devices  16 us (3%)
  between operations  13.7 us (2%)
    all_gather x1, waiting for transfers between devices, per_device(): lax.all_gather(columns, 'stn', axis=3, tiled=True)  262 us
    all_to_all x1, waiting for transfers between devices, per_device(): lax.all_to_all(branch, 'chan', split_axis=0, concat_axis=1, tiled=True)  94.6 us
    dot_general x1, matrix products, per_device(): jnp.einsum(vis_form, left_side, lax.all_gather(columns, 'stn', axis=3, ti...  31.3 us
    dot_general x1, matrix products, per_device(): jnp.einsum('rvcfi,ruvcd->uvfdi', inner, twist_table, precision=better, pr...  25 us
    dot_general x1, matrix products, per_device(): jnp.einsum(phase_form, grouped, band_upper, preferred_element_type=jnp.fl...  16.7 us
    all_to_all x1, starting transfers between devices, per_device(): lax.all_to_all(branch, 'chan', split_axis=0, concat_axis=1, tiled=True)  16 us
    another operation x2, local copies, waits for them, and re-layouts, per_device(): left_side = jnp.stack([columns, swapped], axis=2)  15 us
    dot_general x1, matrix products, per_device(): jnp.einsum('ifqr,qvc->rvcfi', folded, short_table, precision=better, pref...  14.2 us
  transfers between devices with their start and end apart: 2, of which 2 were waited for; matrix products, arithmetic and copies ran while one was open for 4% of the time, Pallas kernels for 0%

commit v1 on v0

--- a/solution.py
+++ b/solution.py
@@ -87,7 +87,10 @@
     )
     band_table = complex_table(band_re, band_im, 1)
     band_upper, band_lower = split_pair(band_table)
-    turned = lax.all_to_all(branch, "chan", split_axis=0, concat_axis=1, tiled=True)
+    turned = jnp.concatenate(
+        lax.all_to_all(jnp.stack(jnp.split(branch, lax.axis_size("chan"), axis=0)), "chan", 0, 0),
+        axis=1,
+    )
     span_len = turned.shape[0]
     sources = turned.shape[1]
     item_count = turned.shape[2]

time: 566 us -> 601 us (1.062)
  local copies, waits for them, and re-layouts: 55.6 us -> 101 us
  starting transfers between devices: 16 us -> 5.45 us
    split x0 -> x1, local copies, waits for them, and re-layouts: none -> 39.5 us  [per_device(): jnp.split(branch, lax.axis_size('chan'), axis=0)]
    all_to_all x1, starting transfers between devices: 16 us -> 5.2 us  [per_device(): lax.all_to_all(jnp.stack(jnp.split(branch, lax.axis_size('chan'), axis=0)...]
    convert_element_type x1 -> x0, local copies, waits for them, and re-layouts: 8.52 us -> none  [per_device(): branch.reshape(slot_count, 1, frames_dev, 2, inputs_dev)]
    another operation x0 -> x2, local copies, waits for them, and re-layouts: none -> 7.86 us  [per_device(): jnp.stack(jnp.split(branch, lax.axis_size('chan'), axis=0))]
    unnamed x4 -> x13, local copies, waits for them, and re-layouts: 10 us -> 16.9 us
where the time goes in v1:
time: 601 us; the launch traced here: 595 us
  waiting for transfers between devices  356 us (59%)
  local copies, waits for them, and re-layouts  101 us (17%)
  matrix products  100 us (17%)
  other arithmetic  17.7 us (3%)
  between operations  14.1 us (2%)
    all_gather x1, waiting for transfers between devices, per_device(): lax.all_gather(columns, 'stn', axis=3, tiled=True)  262 us
    all_to_all x1, waiting for transfers between devices, per_device(): lax.all_to_all(jnp.stack(jnp.split(branch, lax.axis_size('chan'), axis=0)...  94.2 us
    split x1, local copies, waits for them, and re-layouts, per_device(): jnp.split(branch, lax.axis_size('chan'), axis=0)  39.5 us
    dot_general x1, matrix products, per_device(): jnp.einsum(vis_form, left_side, lax.all_gather(columns, 'stn', axis=3, ti...  31.3 us
    dot_general x1, matrix products, per_device(): jnp.einsum('rvcfi,ruvcd->uvfdi', inner, twist_table, precision=better, pr...  25.1 us
    dot_general x1, matrix products, per_device(): jnp.einsum(phase_form, grouped, band_upper, preferred_element_type=jnp.fl...  17 us
    unnamed x13, local copies, waits for them, and re-layouts  16.9 us
    another operation x2, local copies, waits for them, and re-layouts, per_device(): left_side = jnp.stack([columns, swapped], axis=2)  15 us
  transfers between devices with their start and end apart: 2, of which 2 were waited for; matrix products, arithmetic and copies ran while one was open for 4% of the time, Pallas kernels for 0%

profile of v1, /device:TPU:0, one launch (start us, length us, event | category | flops | bytes accessed | tf_op | source)
XLA Modules:
  0.0 594.6 jit_solution(12672252521858460353)
XLA Ops:
  6.5 0.3 fusion.36
  6.9 0.2 fusion.38
  7.1 0.5 copy.208
  7.6 0.5 copy.209
  8.1 6.8 %copy.210 = bf16[256,1,8,1024]{0,3,2,1:T(8,128)(2,1)} copy(bf16[256,1,8,1024]{3,2,1,0:T(8,128)(2,1)} %param.2) | data formatting | bytes 8388608 | tf_op args[0]
  15.0 1.1 constant_dynamic-slice_fusion.6
  16.0 12.3 %multiply_bitcast_fusion = f32[256,8,128,8]{0,3,2,1:T(8,128)} fusion(bf16[256,8,1024]{0,2,1:T(8,128)(2,1)} %bitcast.109, f32[8]{0:T(128)S(1)} %compare_convert_fusion, f32[1024]{0:T(1024)S(1)} %bitcast.120, f32[1024]{0:T(1024)S(1)} %bitcast.114, f32[1024]{0:T(1024)S(1)} %bitcast.115, f32[1024]{0:T(1024)S(1)} %bitcast.116, f32[1024]{0:T(1024)S(1)} %bitcast.117, ...), kind=kLoop, calls=%fused_computation.24 | loop fusion | flops 50331648 | bytes 12615712 | tf_op jit(solution)/shard_map/reshape | solution.py:63
  28.4 9.2 %copy.211 = f32[256,8,128,8]{2,0,3,1:T(8,128)} copy(f32[256,8,128,8]{0,3,2,1:T(8,128)} %multiply_bitcast_fusion) | data formatting | bytes 16777216 | tf_op jit(solution)/shard_map/reshape | solution.py:63
  37.5 14.1 %fusion.18 = f32[8,128,2,8,256,1]{4,1,0,3,2,5:T(8,128)} fusion(f32[256,8,128,8]{2,0,3,1:T(8,128)} %copy.211, f32[128,128,1]{0,1,2:T(8,128)S(1)} %get-tuple-element.32, f32[128,128,1]{0,1,2:T(8,128)S(1)} %get-tuple-element.33), kind=kOutput, calls=%fused_computation.27 | convolution fusion | flops 3221258240 | bytes 25296896 | tf_op jit(solution)/shard_map/ifqr,qvc->rvcfi/dot_general | solution.py:67
  51.6 25.1 %fusion.3 = bf16[8,128,8,2,256]{4,0,2,3,1:T(8,128)(2,1)} fusion(f32[8,128,2,8,256,1]{4,1,0,3,2,5:T(8,128)} %fusion.18, f32[8,8,128,1,2]{0,1,3,4,2:T(8,128)S(1)} %bitcast.112, f32[8,8,128,1,2]{0,1,3,4,2:T(8,128)S(1)} %bitcast.111), kind=kOutput, calls=%fused_computation.12 | convolution fusion | flops 406880256 | bytes 25296896 | tf_op jit(solution)/shard_map/rvcfi,ruvcd->uvfdi/dot_general | solution.py:76
  76.7 39.5 %fusion.58 = (bf16[1,128,8,2,256]{4,0,2,3,1:T(2,128)(2,1)S(1)}, bf16[1,128,8,2,256]{4,0,2,3,1:T(2,128)(2,1)S(1)}, bf16[1,128,8,2,256]{4,0,2,3,1:T(2,128)(2,1)S(1...) fusion(bf16[8,128,8,2,256]{4,0,2,3,1:T(8,128)(2,1)} %fusion.3), kind=kLoop, calls=%fused_computation.100 | loop fusion | bytes 16777216 | tf_op jit(solution)/shard_map/split | solution.py:91
  116.2 0.0 copy-start.1
  116.2 2.0 bitcast_dynamic-update-slice_fusion.7
  118.3 1.9 bitcast_dynamic-update-slice_fusion.6
  120.1 1.9 bitcast_dynamic-update-slice_fusion.5
  122.0 0.0 copy-done.1
  122.0 0.3 bitcast_dynamic-update-slice_fusion.4
  122.3 0.3 bitcast_dynamic-update-slice_fusion.3
  122.6 0.3 bitcast_dynamic-update-slice_fusion.2
  122.9 0.3 bitcast_dynamic-update-slice_fusion.1
  123.2 0.3 bitcast_dynamic-update-slice_fusion
  123.5 7.6 %copy.213 = bf16[8,128,1,8,2,256]{5,4,3,1,2,0:T(2,128)(2,1)} copy(bf16[8,128,1,8,2,256]{5,3,4,2,1,0:T(8,128)(2,1)S(1)} %bitcast_dynamic-update-slice_fusion) | data formatting | bytes 16777216 | tf_op jit(solution)/shard_map/stack | solution.py:91
  131.1 5.2 all-to-all-start
  136.3 0.2 all-gather.2.cloned.1.call-start
  136.5 0.1 fusion.52
  136.6 0.1 fusion.50
  136.7 94.2 %all-to-all-done = bf16[8,128,1,8,2,256]{5,4,3,1,2,0:T(2,128)(2,1)} async-done(((bf16[8,128,1,8,2,256]{5,4,3,1,2,0:T(2,128)(2,1)}), bf16[8,128,1,8,2,256]{5,4,3,1,2,0:T(2,128)(2,1)}, u32[]{:S(2)}, u32[]{:S(2)}) %all-to-all-start) | async-done | bytes 8388640 | tf_op jit(solution)/shard_map/all_to_all | solution.py:91
  230.8 12.5 %fusion.8 = f32[4,2,128,8,256,1]{4,0,5,3,2,1:T(4,128)} fusion(bf16[8,128,1,8,2,256]{5,4,3,1,2,0:T(2,128)(2,1)} %all-to-all-done, f32[8,1,4,2]{0,2,1,3:T(4,128)S(1)} %get-tuple-element.29, f32[8,1,4,2]{0,2,1,3:T(4,128)S(1)} %get-tuple-element.28), kind=kOutput, calls=%fused_computation.18 | convolution fusion | flops 67109504 | bytes 16777728 | tf_op jit(solution)/shard_map/wgpfci,pcbd->bwgfdi/dot_general | solution.py:101
  243.4 17.0 %fusion.7 = bf16[4,2,128,8,256]{4,0,3,2,1:T(4,128)(2,1)} fusion(f32[4,2,128,8,256,1]{4,0,5,3,2,1:T(4,128)} %fusion.8, bf16[8,128,1,8,2,256]{5,4,3,1,2,0:T(2,128)(2,1)} %all-to-all-done, f32[8,1,4,2]{0,2,1,3:T(4,128)S(1)} %get-tuple-element.29, f32[8,1,4,2]{0,2,1,3:T(4,128)S(1)} %get-tuple-element.28), kind=kOutput, calls=%fused_computation.17 | convolution fusion | flops 71303680 | bytes 20972032 | tf_op jit(solution)/shard_map/wgpfci,pcbd->bwgfdi/dot_general | solution.py:99
  260.4 4.3 copy.215
  264.7 0.0 copy-start
  264.7 2.0 copy-done
  266.7 2.8 copy.221
  269.4 0.0 all-gather.2.cloned.1.call-update
  269.4 7.5 %copy.218 = bf16[4,8,1,256,256]{3,4,2,1,0:T(8,128)(2,1)} copy(bf16[4,8,1,256,256]{4,0,3,1,2:T(4,128)(2,1)} %bitcast.108) | data formatting | bytes 8388608 | tf_op jit(solution)/shard_map/stack;reshape;reshape | solution.py:110
  276.9 3.9 fusion.59
  280.8 1.2 copy.241
  282.0 2.4 copy_negate_fusion
  284.4 2.3 pad_maximum_fusion
  286.8 7.5 %copy.219 = bf16[4,8,1,256,256]{3,4,2,1,0:T(8,128)(2,1)} copy(bf16[4,8,1,256,256]{4,1,3,0,2:T(8,128)(2,1)} %bitcast.110) | data formatting | bytes 8388608 | tf_op jit(solution)/shard_map/stack;reshape | solution.py:110
  294.3 261.7 %all-gather.2.cloned.1.call-done = bf16[4,8,256,1024]{3,2,1,0:T(8,128)(2,1)} async-done(((bf16[4,8,256,256]{3,2,1,0:T(8,128)(2,1)}), bf16[4,8,256,1024]{3,2,1,0:T(8,128)(2,1)}) %all-gather.2.cloned.1.call-update) | async-done | bytes 16777232 | tf_op jit(solution)/shard_map/all_gather | solution.py:118
  556.0 31.3 %convolution_multiply_fusion = f32[4,8,2,256,1024]{4,3,2,1,0:T(8,128)} fusion(bf16[4,8,256,1024]{3,2,1,0:T(8,128)(2,1)} %all-gather.2.cloned.1.call-done, bf16[4,8,1,256,256]{3,4,2,1,0:T(8,128)(2,1)} %copy.219, bf16[4,8,1,256,256]{3,4,2,1,0:T(8,128)(2,1)} %copy.218), kind=kOutput, calls=%fused_computation | convolution fusion | flops 8610906112 | bytes 92274688 | tf_op jit(solution)/shard_map/bsokn,bskw->bsonw/dot_general | solution.py:115
  (5 shorter events, 0.0 us)
Async XLA Ops:
  116.2 5.8 copy-start.1
  131.1 99.7 %all-to-all-start = ((bf16[8,128,1,8,2,256]{5,4,3,1,2,0:T(2,128)(2,1)}), bf16[8,128,1,8,2,256]{5,4,3,1,2,0:T(2,128)(2,1)}, u32[]{:S(2)}, u32[]{:S(2)}) async-start(bf16[8,128,1,8,2,256]{5,4,3,1,2,0:T(2,128)(2,1)} %copy.213), calls=%async_computation | async-start | bytes 16777216 | tf_op jit(solution)/shard_map/all_to_all | solution.py:91
  136.3 419.7 %all-gather.2.cloned.1.call-start = ((), (), s32[]{:S(2)}) async-start(), calls=%async_computation.1 | async-start | bytes 20971520 | tf_op jit(solution)/shard_map/all_gather | solution.py:118
  264.7 2.0 copy-start
Sparse Core Ops, SparseCore 0:
  269.6 286.3 all-gather.1
